TPU v7x, 256 devices: a whole 4x4x8 slice. The times are simulated.
256 devices in a mesh: blk: 32 (over y_lo, z, core), head: 8 (over x, y_hi).
Axes of the slice: x: 4, y: 4 (y_hi: 2, y_lo: 2; y = y_hi * 2 + y_lo), z: 8, core: 2. Of those that a mesh axis runs over, the one named last changes fastest.
Arguments:
- pages: bfloat16 [32, 16, 16, 768], P('blk'), may hold values from -6 to 6
- valid_counts: int32 [32], replicated, may hold values from 32 to 256
- dw_weight: float32 [7, 7, 768], replicated, may hold values from -0.875 to 0.875
- dw_bias: float32 [768], replicated, may hold values from -3 to 3
- norm1_gain: float32 [768], replicated, may hold values from 0.5 to 2
- fc1_w: bfloat16 [768, 3072], P(None, 'head'), may hold values from -0.21875 to 0.21875
- fc1_b: float32 [3072], P('head'), may hold values from -3 to 3
- fc2_w: bfloat16 [3072, 768], P('head'), may hold values from -0.109375 to 0.109375
- fc2_b: float32 [768], replicated, may hold values from -3 to 3
- layer_scale: float32 [768], replicated, may hold values from 0.5 to 2
- norm2_gain: float32 [768], replicated, may hold values from 0.5 to 2
- w_query: bfloat16 [768, 4096], P(None, 'head'), may hold values from -3 to 3
- w_key: bfloat16 [768, 1024], P(None, 'head'), may hold values from -0.21875 to 0.21875
- w_value: bfloat16 [768, 1024], P(None, 'head'), may hold values from -0.21875 to 0.21875
- w_out: bfloat16 [4096, 768], P('head'), may hold values from -0.09375 to 0.09375
Outputs:
- mixed: bfloat16 [8192, 768], P(('blk', 'head'))
All inputs are finite; a program needn't handle non-finite values.
Results may differ from a plain program's by a relative error of at most 0.023.
Values may be sent and summed in bfloat16 or wider, within the bound.
No kernel may reach another device: no remote copies, remote signals or barrier semaphores. Data moves between devices by JAX's collectives and lax.ppermute only.
A program may use at most 128 MiB of HBM per device.

v0:
```python
import jax
import jax.numpy as jnp
from jax import lax
from jax.sharding import PartitionSpec as P

HEADS = 32
KV_HEADS = 8
HD = 128


def depthwise(pages, dw_weight, dw_bias):
    height = pages.shape[1]
    breadth = pages.shape[2]
    padded = jnp.pad(pages.astype(jnp.float32), ((0, 0), (3, 3), (3, 3), (0, 0)))
    total = jnp.zeros(pages.shape, jnp.float32)
    for vertical in range(7):
        for sideways in range(7):
            total = (
                total
                + padded[:, vertical : vertical + height, sideways : sideways + breadth, :]
                * dw_weight[vertical, sideways]
            )
    return total + dw_bias


def layer_norm(values, gain, epsilon):
    centred = values - jnp.mean(values, axis=-1, keepdims=True)
    spread = jnp.mean(centred * centred, axis=-1, keepdims=True)
    return centred * lax.rsqrt(spread + epsilon) * gain


def mlp_partial(pages, dw_weight, dw_bias, norm1_gain, fc1_w, fc1_b, fc2_w):
    convolved = depthwise(pages, dw_weight, dw_bias)
    flattened = convolved.reshape(-1, convolved.shape[-1])
    normed = layer_norm(flattened, norm1_gain, 1e-06).astype(jnp.bfloat16)
    hidden = jax.nn.gelu(
        jnp.dot(normed, fc1_w, preferred_element_type=jnp.float32) + fc1_b, approximate=False
    ).astype(jnp.bfloat16)
    return jnp.dot(hidden, fc2_w, preferred_element_type=jnp.float32)


def fold_keys(carry, keys, values, queries, valid_counts, page_tokens):
    running_top, denominator, weighted = carry
    count = keys.shape[0]
    kv_groups = queries.shape[1]
    key_heads = keys.reshape(count, kv_groups, HD)
    value_heads = values.reshape(count, kv_groups, HD)
    scores = jnp.einsum(
        "rgqd,ngd->gqrn", queries, key_heads, preferred_element_type=jnp.float32
    ) * HD ** (-0.5)
    position = jnp.arange(count, dtype=jnp.int32)
    page_number = position // page_tokens
    matches = page_number[:, None] == jnp.arange(valid_counts.shape[0], dtype=jnp.int32)[None, :]
    page_count = jnp.sum(jnp.where(matches, valid_counts[None, :], 0), axis=1)
    valid = position % page_tokens < page_count
    scores = jnp.where(valid, scores, -1e30)
    new_top = jnp.maximum(running_top, jnp.max(scores, axis=-1))
    exponent = jnp.where(valid, jnp.exp(scores - new_top[..., None]), 0.0)
    denominator = jnp.sum(exponent, axis=-1)
    update = jnp.einsum(
        "gqrn,ngd->gqrd",
        exponent.astype(jnp.bfloat16),
        value_heads,
        preferred_element_type=jnp.float32,
    )
    weighted = update
    return (new_top, denominator, weighted)


def per_device(
    pages,
    valid_counts,
    dw_weight,
    dw_bias,
    norm1_gain,
    fc1_w,
    fc1_b,
    fc2_w,
    fc2_b,
    layer_scale,
    norm2_gain,
    w_query,
    w_key,
    w_value,
    w_out,
):
    channels = pages.shape[-1]
    page_tokens = pages.shape[1] * pages.shape[2]
    rows = pages.shape[0] * page_tokens
    partial_sum = mlp_partial(pages, dw_weight, dw_bias, norm1_gain, fc1_w, fc1_b, fc2_w)
    flat_pages = pages.reshape(rows, channels)
    summed = lax.psum(partial_sum, "head")
    block = flat_pages.astype(jnp.float32) + layer_scale * (summed + fc2_b)
    normed = layer_norm(block, norm2_gain, 1e-05).astype(jnp.bfloat16)
    kv_groups = w_key.shape[1] // HD
    group = HEADS // KV_HEADS
    queries = jnp.dot(normed, w_query, preferred_element_type=jnp.float32).astype(jnp.bfloat16)
    queries = queries.reshape(rows, kv_groups, group, HD)
    initial = (
        jnp.full((kv_groups, group, rows), -1e30, jnp.float32),
        jnp.zeros((kv_groups, group, rows), jnp.float32),
        jnp.zeros((kv_groups, group, rows, HD), jnp.float32),
    )
    own_keys = jnp.dot(normed, w_key, preferred_element_type=jnp.float32).astype(jnp.bfloat16)
    own_values = jnp.dot(normed, w_value, preferred_element_type=jnp.float32).astype(jnp.bfloat16)
    final = fold_keys(
        initial,
        lax.all_gather(own_keys, "blk", axis=0, tiled=True),
        lax.all_gather(own_values, "blk", axis=0, tiled=True),
        queries,
        valid_counts,
        page_tokens,
    )
    attended = (final[2] / final[1][..., None]).astype(jnp.bfloat16)
    attended = attended.transpose(2, 0, 1, 3).reshape(rows, kv_groups * group * HD)
    mixed = lax.psum_scatter(
        jnp.dot(attended, w_out, preferred_element_type=jnp.float32),
        "head",
        scatter_dimension=0,
        tiled=True,
    )
    return mixed.astype(jnp.bfloat16)


def solution(mesh):
    in_specs = (
        P("blk", None, None, None),
        P(),
        P(),
        P(),
        P(),
        P(None, "head"),
        P("head"),
        P("head", None),
        P(),
        P(),
        P(),
        P(None, "head"),
        P(None, "head"),
        P(None, "head"),
        P("head", None),
    )
    out_specs = P(("blk", "head"), None)
    return jax.shard_map(
        per_device, mesh=mesh, in_specs=in_specs, out_specs=out_specs, check_vma=False
    )
```

profile of v0, /device:TPU:2, one launch (start us, length us, event | category | flops | bytes accessed | tf_op | source)
XLA Modules:
  0.0 354.3 jit_solution(8926439461209473395)
XLA Ops:
  6.5 0.0 copy-start
  6.5 0.0 all-reduce.3.cloned.1.call-start
  6.5 1.3 slice_reduce_fusion.48
  7.9 1.4 slice_reduce_fusion.47
  9.3 1.1 slice_reduce_fusion.46
  10.4 1.1 convert_element_type.54
  11.5 7.0 %fusion.207 = (f32[16,16]{1,0:T(8,128)S(1)}, f32[1,16,16,768]{3,2,1,0:T(8,128)S(1)}) fusion(f32[768]{0:T(1024)} %param.18, f32[768]{0:T(1024)S(1)} %get-tuple-element.52, f32[768]{0:T(1024)S(1)} %get-tuple-element.53, f32[768]{0:T(1024)S(1)} %get-tuple-element.6, f32[768]{0:T(1024)S(1)} %get-tuple-element.7, f32[768]{0:T(1024)S(1)} %get-tuple-element.8, ...), kind=kLoop, calls=%fused_computation.328 | loop fusion | flops 19463936 | bytes 1727488 | tf_op jit(solution)/shard_map/reduce_sum | solution.py:27
  18.5 0.1 div.34
  18.6 0.2 multiply_reduce_fusion.1
  18.8 0.1 rsqrt.20
  18.9 0.9 fusion.122
  19.8 3.6 %fusion.133 = f32[256,768]{1,0:T(8,128)} fusion(bf16[384,768]{1,0:T(8,128)(2,1)} %param.22, bf16[256,768]{1,0:T(8,128)(2,1)S(1)} %fusion.122, bf16[768,384]{1,0:T(8,128)(2,1)} %param.20, f32[384]{0:T(512)} %param.21), kind=kOutput, calls=%fused_computation.195 | convolution fusion | flops 308477952 | bytes 2360832 | tf_op jit(solution)/shard_map/dot_general | solution.py:39
  23.4 0.0 all-reduce.3.cloned.1.call-update
  23.4 0.0 all-gather.3.cloned.1.call-start
  23.4 93.7 %all-reduce.3.cloned.1.call-done = f32[256,768]{1,0:T(8,128)} async-done(((f32[256,768]{1,0:T(8,128)}), f32[256,768]{1,0:T(8,128)}) %all-reduce.3.cloned.1.call-update) | async-done | bytes 786448 | tf_op jit(solution)/shard_map/psum | solution.py:92
  117.2 1.5 fusion.167
  118.6 1.5 multiply_reduce_fusion
  120.2 1.5 multiply_convert_fusion
  121.7 1.8 convolution_convert_fusion.2
  123.5 0.0 all-gather.3.cloned.1.call-update
  123.5 0.0 all-gather.5.cloned.1.call-start
  123.6 0.9 select_reduce_fusion
  124.5 1.5 fusion.12
  126.0 1.9 convolution_convert_fusion.1
  127.9 0.0 all-gather.5.cloned.1.call-update
  127.9 0.2 reduce-scatter.2.cloned.1.call-start
  128.1 59.5 %all-gather.3.cloned.1.call-done = bf16[8192,128]{1,0:T(8,128)(2,1)} async-done(((bf16[256,128]{1,0:T(8,128)(2,1)}), bf16[8192,128]{1,0:T(8,128)(2,1)}) %all-gather.3.cloned.1.call-update) | async-done | bytes 2097168 | tf_op jit(solution)/shard_map/all_gather | solution.py:108
  187.6 14.5 %bitcast_reduce_fusion = (f32[4,256]{1,0:T(4,128)S(1)}, f32[8192,256,4]{1,0,2:T(8,128)}) fusion(pred[8192]{0:T(1024)(128)(4,1)S(1)} %fusion.168, bf16[32,4,8,128]{3,2,1,0:T(8,128)(2,1)S(1)} %fusion.12, bf16[8192,128]{1,0:T(8,128)(2,1)} %all-gather.3.cloned.1.call-done), kind=kOutput, calls=%fused_computation.1 | convolution fusion | flops 2172648448 | bytes 35926016 | tf_op jit(solution)/shard_map/rgqd,ngd->gqrn/dot_general | solution.py:48
  202.1 15.1 %fusion.2 = f32[4,256]{1,0:T(4,128)S(1)} fusion(f32[8192,256,4]{1,0,2:T(8,128)} %get-tuple-element.57, f32[4,256]{1,0:T(4,128)S(1)} %broadcast_maximum_fusion, pred[8192]{0:T(1024)(128)(4,1)S(1)} %fusion.168), kind=kLoop, calls=%fused_computation.5 | loop fusion | flops 41942016 | bytes 33570816 | tf_op jit(solution)/shard_map/reduce_sum | solution.py:59
  217.3 38.0 %all-gather.5.cloned.1.call-done = bf16[8192,128]{0,1:T(8,128)(2,1)} async-done(((bf16[256,128]{0,1:T(8,128)(2,1)}), bf16[8192,128]{0,1:T(8,128)(2,1)}) %all-gather.5.cloned.1.call-update) | async-done | bytes 2097168 | tf_op jit(solution)/shard_map/all_gather | solution.py:109
  255.2 14.3 %fusion.18 = bf16[4,256,128]{1,2,0:T(8,128)(2,1)S(1)} fusion(f32[8192,256,4]{1,0,2:T(8,128)} %get-tuple-element.57, f32[4,256]{1,0:T(4,128)S(1)} %broadcast_maximum_fusion, pred[8192]{0:T(1024)(128)(4,1)S(1)} %fusion.168, bf16[8192,128]{0,1:T(8,128)(2,1)} %all-gather.5.cloned.1.call-done, f32[4,256]{1,0:T(4,128)S(1)} %fusion.2), kind=kOutput, calls=%fused_computation.70 | convolution fusion | flops 2189688832 | bytes 35930112 | tf_op jit(solution)/shard_map/gqrn,ngd->gqrd/dot_general | solution.py:60
  269.5 0.0 copy-done
  269.6 1.3 fusion.209
  270.8 0.0 reduce-scatter.2.cloned.1.call-update
  270.8 75.4 %reduce-scatter.2.cloned.1.call-done = f32[32,768]{1,0:T(8,128)} async-done(((f32[256,768]{1,0:T(8,128)}), f32[32,768]{1,0:T(8,128)}) %reduce-scatter.2.cloned.1.call-update) | async-done | bytes 98320 | tf_op jit(solution)/shard_map/reduce_scatter | solution.py:116
  346.2 1.5 convert_element_type.53
  (7 shorter events, 0.0 us)
Async XLA Ops:
  6.5 263.0 %copy-start = (bf16[512,768]{1,0:T(8,128)(2,1)S(1)}, bf16[512,768]{1,0:T(8,128)(2,1)}, u32[]{:S(2)}) copy-start(bf16[512,768]{1,0:T(8,128)(2,1)} %param.29) | copy-start | bytes 2359300
  6.5 110.6 %all-reduce.3.cloned.1.call-start = ((), (), s32[]{:S(2)}) async-start(), calls=%async_computation.1 | async-start | bytes 1572864 | tf_op jit(solution)/shard_map/psum | solution.py:92
  23.4 164.2 %all-gather.3.cloned.1.call-start = ((), (), s32[]{:S(2)}) async-start(), calls=%async_computation.2 | async-start | bytes 2162688 | tf_op jit(solution)/shard_map/all_gather | solution.py:108
  123.5 131.7 %all-gather.5.cloned.1.call-start = ((), (), s32[]{:S(2)}) async-start(), calls=%async_computation.3 | async-start | bytes 2162688 | tf_op jit(solution)/shard_map/all_gather | solution.py:109
  127.9 218.4 %reduce-scatter.2.cloned.1.call-start = ((), (), s32[]{:S(2)}) async-start(), calls=%async_computation.4 | async-start | bytes 884736 | tf_op jit(solution)/shard_map/reduce_scatter | solution.py:116
Sparse Core Ops, SparseCore 0:
  23.5 93.5 all-reduce.2
  123.6 63.9 all-gather.2
  189.5 65.6 all-gather.4
  271.0 75.2 reduce-scatter.1
where the time goes:
time: 355 us; the launch traced here: 354 us
  waiting for transfers between devices  267 us (75%)
  matrix products  38.8 us (11%)
  other arithmetic  31.2 us (9%)
  between operations  13.2 us (4%)
  local copies, waits for them, and re-layouts  4.04 us (1%)
    psum x1, waiting for transfers between devices, per_device(): summed = lax.psum(partial_sum, 'head')  93.7 us
    reduce_scatter x1, waiting for transfers between devices, per_device(): lax.psum_scatter(jnp.dot(attended, w_out, preferred_element_type=jnp.floa...  75.4 us
    all_gather x1, waiting for transfers between devices, per_device(): lax.all_gather(own_keys, 'blk', axis=0, tiled=True)  59.5 us
    all_gather x1, waiting for transfers between devices, per_device(): lax.all_gather(own_values, 'blk', axis=0, tiled=True)  38 us
    reduce_sum x1, other arithmetic, fold_keys(): denominator = jnp.sum(exponent, axis=-1)  15.1 us
    dot_general x1, matrix products, fold_keys(): jnp.einsum('rgqd,ngd->gqrn', queries, key_heads, preferred_element_type=j...  14.5 us
    dot_general x1, matrix products, fold_keys(): jnp.einsum('gqrn,ngd->gqrd', exponent.astype(jnp.bfloat16), value_heads,...  14.3 us
    reduce_sum x2, other arithmetic, layer_norm(): centred = values - jnp.mean(values, axis=-1, keepdims=True)  8.47 us
  transfers between devices with their start and end apart: 4, of which 4 were waited for; matrix products, arithmetic and copies ran while one was open for 10% of the time, Pallas kernels for 0%

commit v1 on v0

--- a/solution.py
+++ b/solution.py
@@ -105,7 +105,9 @@
     own_values = jnp.dot(normed, w_value, preferred_element_type=jnp.float32).astype(jnp.bfloat16)
     final = fold_keys(
         initial,
-        lax.all_gather(own_keys, "blk", axis=0, tiled=True),
+        jnp.concatenate(
+            lax.all_to_all(jnp.stack([own_keys] * lax.axis_size("blk")), "blk", 0, 0), axis=0
+        ),
         lax.all_gather(own_values, "blk", axis=0, tiled=True),
         queries,
         valid_counts,

time: 355 us -> 316 us (0.89)
  waiting for transfers between devices: 267 us -> 222 us
  starting transfers between devices: 0.31 us -> 7.69 us
    all_gather x1 -> x0, waiting for transfers between devices: 59.5 us -> none  [per_device(): lax.all_gather(own_keys, 'blk', axis=0, tiled=True)]
    all_to_all x0 -> x1, waiting for transfers between devices: none -> 50.6 us  [per_device(): lax.all_to_all(jnp.stack([own_keys] * lax.axis_size('blk')), 'blk', 0, 0)]
    all_gather x1, waiting for transfers between devices: 38 us -> 1.41 us  [per_device(): lax.all_gather(own_values, 'blk', axis=0, tiled=True)]
    all_to_all x0 -> x1, starting transfers between devices: none -> 7.43 us  [per_device(): lax.all_to_all(jnp.stack([own_keys] * lax.axis_size('blk')), 'blk', 0, 0)]
where the time goes in v1:
time: 316 us
  waiting for transfers between devices  222 us (70%)
  matrix products  35.7 us (11%)
  other arithmetic  31.2 us (10%)
  between operations  13.2 us (4%)
  starting transfers between devices  7.69 us (2%)
  local copies, waits for them, and re-layouts  5.9 us (2%)
    psum x1, waiting for transfers between devices, per_device(): summed = lax.psum(partial_sum, 'head')  93.7 us
    reduce_scatter x1, waiting for transfers between devices, per_device(): lax.psum_scatter(jnp.dot(attended, w_out, preferred_element_type=jnp.floa...  76 us
    all_to_all x1, waiting for transfers between devices, per_device(): lax.all_to_all(jnp.stack([own_keys] * lax.axis_size('blk')), 'blk', 0, 0)  50.6 us
    reduce_sum x1, other arithmetic, fold_keys(): denominator = jnp.sum(exponent, axis=-1)  15.1 us
    dot_general x1, matrix products, fold_keys(): jnp.einsum('gqrn,ngd->gqrd', exponent.astype(jnp.bfloat16), value_heads,...  14.3 us
    dot_general x1, matrix products, fold_keys(): jnp.einsum('rgqd,ngd->gqrn', queries, key_heads, preferred_element_type=j...  12.1 us
    reduce_sum x2, other arithmetic, layer_norm(): centred = values - jnp.mean(values, axis=-1, keepdims=True)  8.47 us
    all_to_all x1, starting transfers between devices, per_device(): lax.all_to_all(jnp.stack([own_keys] * lax.axis_size('blk')), 'blk', 0, 0)  7.43 us
  transfers between devices with their start and end apart: 4, of which 4 were waited for; matrix products, arithmetic and copies ran while one was open for 10% of the time, Pallas kernels for 0%

profile of v1, /device:TPU:2, one launch (start us, length us, event | category | flops | bytes accessed | tf_op | source)
XLA Modules:
  0.0 315.6 jit_solution(14187767594226010919)
XLA Ops:
  6.5 0.0 copy-start
  6.5 0.0 all-reduce.3.cloned.1.call-start
  6.5 1.4 slice_reduce_fusion.48
  7.9 1.4 slice_reduce_fusion.47
  9.3 1.1 slice_reduce_fusion.46
  10.4 1.1 convert_element_type.54
  11.5 7.0 %fusion.206 = (f32[16,16]{1,0:T(8,128)S(1)}, f32[1,16,16,768]{3,2,1,0:T(8,128)S(1)}) fusion(f32[768]{0:T(1024)} %param.18, f32[768]{0:T(1024)S(1)} %get-tuple-element.52, f32[768]{0:T(1024)S(1)} %get-tuple-element.53, f32[768]{0:T(1024)S(1)} %get-tuple-element.6, f32[768]{0:T(1024)S(1)} %get-tuple-element.7, f32[768]{0:T(1024)S(1)} %get-tuple-element.8, ...), kind=kLoop, calls=%fused_computation.327 | loop fusion | flops 19463936 | bytes 1727488 | tf_op jit(solution)/shard_map/reduce_sum | solution.py:27
  18.5 0.1 div.34
  18.6 0.2 multiply_reduce_fusion.1
  18.9 0.1 rsqrt.20
  18.9 0.9 fusion.120
  19.8 3.6 %fusion.131 = f32[256,768]{1,0:T(8,128)} fusion(bf16[384,768]{1,0:T(8,128)(2,1)} %param.22, bf16[256,768]{1,0:T(8,128)(2,1)S(1)} %fusion.120, bf16[768,384]{1,0:T(8,128)(2,1)} %param.20, f32[384]{0:T(512)} %param.21), kind=kOutput, calls=%fused_computation.193 | convolution fusion | flops 308477952 | bytes 2360832 | tf_op jit(solution)/shard_map/dot_general | solution.py:39
  23.4 0.0 all-reduce.3.cloned.1.call-update
  23.4 93.7 %all-reduce.3.cloned.1.call-done = f32[256,768]{1,0:T(8,128)} async-done(((f32[256,768]{1,0:T(8,128)}), f32[256,768]{1,0:T(8,128)}) %all-reduce.3.cloned.1.call-update) | async-done | bytes 786448 | tf_op jit(solution)/shard_map/psum | solution.py:92
  117.2 1.5 fusion.166
  118.6 1.5 multiply_reduce_fusion
  120.2 1.5 multiply_convert_fusion
  121.7 1.2 convolution_convert_fusion.2
  122.9 1.8 stack.2
  124.7 7.4 %all-to-all-start = ((bf16[32,256,128]{2,1,0:T(8,128)(2,1)}), bf16[32,256,128]{2,1,0:T(8,128)(2,1)S(1)}, u32[]{:S(2)}, u32[]{:S(2)}) async-start(bf16[32,256,128]{2,1,0:T(8,128)(2,1)} %stack.2), calls=%async_computation | async-start | bytes 4194304 | tf_op jit(solution)/shard_map/all_to_all | solution.py:109
  132.1 0.0 all-gather.2.cloned.1.call-start
  132.2 0.9 select_reduce_fusion
  133.1 1.8 convolution_convert_fusion.1
  134.9 0.0 all-gather.2.cloned.1.call-update
  135.0 0.2 reduce-scatter.2.cloned.1.call-start
  135.2 1.5 fusion.10
  136.7 50.6 %all-to-all-done = bf16[32,256,128]{2,1,0:T(8,128)(2,1)S(1)} async-done(((bf16[32,256,128]{2,1,0:T(8,128)(2,1)}), bf16[32,256,128]{2,1,0:T(8,128)(2,1)S(1)}, u32[]{:S(2)}, u32[]{:S(2)}) %all-to-all-start) | async-done | bytes 2097184 | tf_op jit(solution)/shard_map/all_to_all | solution.py:109
  187.3 12.1 %bitcast_reduce_fusion = (f32[4,256]{1,0:T(4,128)S(1)}, f32[8192,256,4]{1,0,2:T(8,128)}) fusion(pred[8192]{0:T(1024)(128)(4,1)S(1)} %fusion.167, bf16[8192,128,1]{1,0,2:T(8,128)(2,1)S(1)} %bitcast.92, bf16[32,4,8,128]{3,2,1,0:T(8,128)(2,1)S(1)} %fusion.10), kind=kOutput, calls=%fused_computation.1 | convolution fusion | flops 2172648448 | bytes 35926016 | tf_op jit(solution)/shard_map/rgqd,ngd->gqrn/dot_general | solution.py:48
  199.4 15.1 %fusion.2 = f32[4,256]{1,0:T(4,128)S(1)} fusion(f32[8192,256,4]{1,0,2:T(8,128)} %get-tuple-element.57, f32[4,256]{1,0:T(4,128)S(1)} %broadcast_maximum_fusion, pred[8192]{0:T(1024)(128)(4,1)S(1)} %fusion.167), kind=kLoop, calls=%fused_computation.5 | loop fusion | flops 41942016 | bytes 33570816 | tf_op jit(solution)/shard_map/reduce_sum | solution.py:59
  214.5 1.4 all-gather.2.cloned.1.call-done
  215.9 14.3 %fusion.16 = bf16[4,256,128]{1,2,0:T(8,128)(2,1)S(1)} fusion(f32[8192,256,4]{1,0,2:T(8,128)} %get-tuple-element.57, f32[4,256]{1,0:T(4,128)S(1)} %broadcast_maximum_fusion, pred[8192]{0:T(1024)(128)(4,1)S(1)} %fusion.167, bf16[8192,128]{0,1:T(8,128)(2,1)} %all-gather.2.cloned.1.call-done, f32[4,256]{1,0:T(4,128)S(1)} %fusion.2), kind=kOutput, calls=%fused_computation.68 | convolution fusion | flops 2189688832 | bytes 35930112 | tf_op jit(solution)/shard_map/gqrn,ngd->gqrd/dot_general | solution.py:60
  230.2 0.0 copy-done
  230.2 1.3 fusion.208
  231.5 0.0 reduce-scatter.2.cloned.1.call-update
  231.5 76.0 %reduce-scatter.2.cloned.1.call-done = f32[32,768]{1,0:T(8,128)} async-done(((f32[256,768]{1,0:T(8,128)}), f32[32,768]{1,0:T(8,128)}) %reduce-scatter.2.cloned.1.call-update) | async-done | bytes 98320 | tf_op jit(solution)/shard_map/reduce_scatter | solution.py:118
  307.5 1.5 convert_element_type.53
  (7 shorter events, 0.0 us)
Async XLA Ops:
  6.5 223.7 %copy-start = (bf16[512,768]{1,0:T(8,128)(2,1)S(1)}, bf16[512,768]{1,0:T(8,128)(2,1)}, u32[]{:S(2)}) copy-start(bf16[512,768]{1,0:T(8,128)(2,1)} %param.29) | copy-start | bytes 2359300
  6.5 110.6 %all-reduce.3.cloned.1.call-start = ((), (), s32[]{:S(2)}) async-start(), calls=%async_computation.2 | async-start | bytes 1572864 | tf_op jit(solution)/shard_map/psum | solution.py:92
  124.7 62.7 %all-to-all-start = ((bf16[32,256,128]{2,1,0:T(8,128)(2,1)}), bf16[32,256,128]{2,1,0:T(8,128)(2,1)S(1)}, u32[]{:S(2)}, u32[]{:S(2)}) async-start(bf16[32,256,128]{2,1,0:T(8,128)(2,1)} %stack.2), calls=%async_computation | async-start | bytes 4194304 | tf_op jit(solution)/shard_map/all_to_all | solution.py:109
  132.1 83.8 %all-gather.2.cloned.1.call-start = ((), (), s32[]{:S(2)}) async-start(), calls=%async_computation.3 | async-start | bytes 2162688 | tf_op jit(solution)/shard_map/all_gather | solution.py:111
  135.0 172.6 %reduce-scatter.2.cloned.1.call-start = ((), (), s32[]{:S(2)}) async-start(), calls=%async_computation.4 | async-start | bytes 884736 | tf_op jit(solution)/shard_map/reduce_scatter | solution.py:118
Sparse Core Ops, SparseCore 0:
  23.5 93.5 all-reduce.2
  135.1 80.8 all-gather.1
  231.6 75.8 reduce-scatter.1
